TPU v7x, 32 devices: a whole 2x2x4 slice. The times are simulated.
32 devices in a mesh: dp: 8 (over y, x, core), mp: 4 (over z).
Axes of the slice: x: 2, y: 2, z: 4, core: 2. Of those that a mesh axis runs over, the one named last changes fastest.
Arguments:
- tokens: bfloat16 [320, 4096], P('dp'), may hold values from -6 to 6
- attn_gain: float32 [4096], replicated, may hold values from 0.1 to 1.9
- head_gain: float32 [4096], replicated, may hold values from 0.1 to 1.9
- qkv_weight: bfloat16 [4096, 3, 4096], P('dp', None, 'mp'), may hold values from -0.09375 to 0.09375
- out_weight: bfloat16 [4096, 4096], P('mp', 'dp'), may hold values from -0.09375 to 0.09375
- head_weight: bfloat16 [4096, 1024], P('mp'), may hold values from -0.09375 to 0.09375
- key_cache: bfloat16 [320, 64, 4096], P('dp', None, 'mp'), may hold values from -400 to 400
- value_cache: bfloat16 [320, 64, 4096], P('dp', None, 'mp'), may hold values from -6 to 6
- parents: int32 [320], P('dp'), may hold values from 0 to 19
- allowed: int32 [320, 2], P('dp'), may hold values from 0 to 7, all different within a row
Outputs:
- new_stream: bfloat16 [320, 4096], P('dp')
- next_logits: float32 [320, 256], P('dp', 'mp')
Inputs may be any that keep to these rules, and one draw needn't show every extreme that they name: `parents`: a beam's parent is a beam of the same query. `allowed`: the 2 block ids of a beam differ.
All inputs are finite; a program needn't handle non-finite values.
Results may differ from a plain program's by a relative error of at most 0.017.
Values may be sent and summed in bfloat16 or wider, within the bound.
No kernel may reach another device: no remote copies, remote signals or barrier semaphores. Data moves between devices by JAX's collectives and lax.ppermute only.
A program may use at most 128 MiB of HBM per device.

v0:
```python
import jax
import jax.numpy as jnp
from jax import lax
from jax.sharding import PartitionSpec as P

HEAD = 128
BEAMS = 20
BLOCK = 128


def root_norm(values, gain_vec):
    float_values = values.astype(jnp.float32)
    factor = lax.rsqrt(jnp.mean(float_values * float_values, axis=-1, keepdims=True) + 1e-06)
    return float_values * factor * gain_vec


def select_blocks(whole_logits, allowed):
    block_count = whole_logits.shape[1] // BLOCK
    block_list = whole_logits.reshape(whole_logits.shape[0], block_count, BLOCK)
    one_hot_rows = (
        allowed[:, :, None] == jnp.arange(block_count, dtype=jnp.int32)[None, None, :]
    ).astype(jnp.float32)
    selected_token = jnp.einsum(
        "ioh,ihp->iop", one_hot_rows, block_list, precision=lax.Precision.HIGHEST
    )
    return selected_token.reshape(whole_logits.shape[0], -1)


def on_device(
    tokens,
    attn_gain,
    head_gain,
    qkv_weight,
    out_weight,
    head_weight,
    key_cache,
    value_cache,
    parents,
    allowed,
):
    row_count = tokens.shape[0]
    normed = root_norm(tokens, attn_gain).astype(jnp.bfloat16)
    spread = lax.all_to_all(normed, "dp", split_axis=1, concat_axis=0, tiled=True)
    depth_part = qkv_weight.shape[0]
    head_width = qkv_weight.shape[2]
    flat_qkv = qkv_weight.reshape(depth_part, 3 * head_width)
    projected = lax.psum_scatter(
        jnp.dot(spread, flat_qkv, preferred_element_type=jnp.float32),
        "dp",
        scatter_dimension=0,
        tiled=True,
    )
    projected = projected.astype(jnp.bfloat16).reshape(row_count, 3, head_width)
    local_heads = head_width // HEAD
    length = key_cache.shape[1] + 1
    source = jnp.arange(row_count, dtype=jnp.int32) // BEAMS * BEAMS + parents
    key_rows = jnp.concatenate(
        [jnp.take(key_cache, source, axis=0), projected[:, 1][:, None]], axis=1
    )
    value_rows = jnp.concatenate(
        [jnp.take(value_cache, source, axis=0), projected[:, 2][:, None]], axis=1
    )
    key_rows = key_rows.reshape(row_count, length, local_heads, HEAD)
    value_rows = value_rows.reshape(row_count, length, local_heads, HEAD)
    queries = projected[:, 0].reshape(row_count, local_heads, HEAD)
    scores = jnp.einsum(
        "thd,tjhd->thj", queries, key_rows, preferred_element_type=jnp.float32
    ) * HEAD ** (-0.5)
    softmax_w = jax.nn.softmax(scores, axis=-1).astype(jnp.bfloat16)
    attention_result = jnp.einsum(
        "thj,tjhd->thd", softmax_w, value_rows, preferred_element_type=jnp.float32
    )
    attention_result = attention_result.astype(jnp.bfloat16).reshape(row_count, head_width)
    partial_value = jnp.dot(
        attention_result,
        lax.all_gather(out_weight, "dp", axis=1, tiled=True),
        preferred_element_type=jnp.float32,
    )
    attn_out = lax.psum(partial_value, "mp")
    stream = tokens.astype(jnp.float32) + attn_out
    head_input = root_norm(stream, head_gain).astype(jnp.bfloat16)
    depth_rows = head_weight.shape[0]
    own_part = lax.dynamic_slice_in_dim(
        head_input, lax.axis_index("mp") * depth_rows, depth_rows, 1
    )
    partial_logits = jnp.dot(own_part, head_weight, preferred_element_type=jnp.float32)
    next_logits = lax.psum_scatter(
        select_blocks(partial_logits, allowed).astype(jnp.bfloat16),
        "mp",
        scatter_dimension=1,
        tiled=True,
    ).astype(jnp.float32)
    return (stream.astype(jnp.bfloat16), next_logits)


def solution(mesh):
    in_specs = (
        P("dp", None),
        P(),
        P(),
        P("dp", None, "mp"),
        P("mp", "dp"),
        P("mp", None),
        P("dp", None, "mp"),
        P("dp", None, "mp"),
        P("dp"),
        P("dp", None),
    )
    out_specs = (P("dp", None), P("dp", "mp"))
    return jax.shard_map(
        on_device, mesh=mesh, in_specs=in_specs, out_specs=out_specs, check_vma=False
    )
```

profile of v0, /device:TPU:0, one launch (start us, length us, event | category | flops | bytes accessed | tf_op | source)
XLA Modules:
  0.0 211.9 jit_solution(16103499963755374255)
XLA Ops:
  7.2 0.0 copy-start
  7.2 1.3 fusion.11
  8.5 1.1 fusion.13
  9.6 0.7 copy.55
  10.4 5.2 %all-to-all-start = ((bf16[40,8,512]{2,0,1:T(8,128)(2,1)}), bf16[40,8,512]{2,0,1:T(8,128)(2,1)S(1)}, u32[]{:S(2)}, u32[]{:S(2)}) async-start(bf16[40,8,512]{2,0,1:T(8,128)(2,1)} %bitcast.32), calls=%async_computation | async-start | bytes 655360 | tf_op jit(solution)/shard_map/all_to_all | solution.py:43
  15.6 0.0 reduce-scatter.5.cloned.1.call-start
  15.6 4.7 %copy.24 = bf16[512,3,1024]{0,2,1:T(8,128)(2,1)} copy(bf16[512,3,1024]{2,0,1:T(8,128)(2,1)} %param.15) | data formatting | bytes 6291456 | tf_op args[3]
  20.3 2.9 %all-to-all-done = bf16[40,8,512]{2,0,1:T(8,128)(2,1)S(1)} async-done(((bf16[40,8,512]{2,0,1:T(8,128)(2,1)}), bf16[40,8,512]{2,0,1:T(8,128)(2,1)S(1)}, u32[]{:S(2)}, u32[]{:S(2)}) %all-to-all-start) | async-done | bytes 327712 | tf_op jit(solution)/shard_map/all_to_all | solution.py:43
  23.2 0.0 copy-start.3
  23.2 5.0 %fusion.35 = f32[320,3072]{1,0:T(8,128)} fusion(bf16[320,512]{1,0:T(8,128)(2,1)S(1)} %bitcast.34, bf16[512,3072]{0,1:T(8,128)(2,1)} %bitcast.33), kind=kOutput, calls=%fused_computation.57 | convolution fusion | flops 1006632960 | bytes 7405568 | tf_op jit(solution)/shard_map/dot_general | solution.py:48
  28.2 0.0 reduce-scatter.5.cloned.1.call-update
  28.2 0.0 all-gather.2.cloned.1.call-start
  28.3 0.7 all-gather.2.cloned.1.call-update
  29.0 0.0 all-reduce.2.cloned.1.call-start
  29.0 0.0 copy-done.3
  29.1 7.2 %gather_fusion = bf16[40,64,1024]{2,1,0:T(8,128)(2,1)} fusion(bf16[40,64,1024]{2,1,0:T(8,128)(2,1)} %param.18, s32[1024]{0:T(1024)S(1)} %pad_clamp_fusion), kind=kCustom, calls=%fused_computation.clone | custom fusion | bytes 10485920 | tf_op jit(solution)/shard_map/jit(_take)/gather | solution.py:58
  36.3 7.6 %gather_fusion.1 = bf16[40,64,1024]{2,1,0:T(8,128)(2,1)} fusion(bf16[40,64,1024]{2,1,0:T(8,128)(2,1)} %param.19, s32[1024]{0:T(1024)S(1)} %pad_clamp_fusion), kind=kCustom, calls=%fused_computation.1.clone | custom fusion | bytes 10485920 | tf_op jit(solution)/shard_map/jit(_take)/gather | solution.py:61
  43.9 9.1 %broadcast_select_fusion.1 = (bf16[40,64,1024]{2,1,0:T(8,128)(2,1)}, bf16[40,64,1024]{2,1,0:T(8,128)(2,1)}) fusion(bf16[40,64,1024]{2,1,0:T(8,128)(2,1)} %gather_fusion, pred[40]{0:T(512)(128)(4,1)S(1)} %get-tuple-element.5, bf16[40,64,1024]{2,1,0:T(8,128)(2,1)} %gather_fusion.1), kind=kLoop, calls=%fused_computation.11 | loop fusion | flops 5242880 | bytes 20971560 | tf_op jit(solution)/shard_map/jit(_take)/select_n | solution.py:58
  52.9 24.6 %reduce-scatter.5.cloned.1.call-done = f32[40,3072]{1,0:T(8,128)} async-done(((f32[320,3072]{1,0:T(8,128)}), f32[40,3072]{1,0:T(8,128)}) %reduce-scatter.5.cloned.1.call-update) | async-done | bytes 491536 | tf_op jit(solution)/shard_map/reduce_scatter | solution.py:47
  77.6 1.1 convert_element_type.34
  78.6 0.4 reshape.54
  79.0 0.3 fusion.32
  79.3 11.1 %pad_maximum_fusion = (bf16[40,65,1024]{2,1,0:T(8,128)(2,1)}, bf16[40,65,1024]{2,1,0:T(8,128)(2,1)}) fusion(bf16[40,1,1024]{2,1,0:T(2,128)(2,1)S(1)} %get-tuple-element.7, bf16[40,64,1024]{2,1,0:T(8,128)(2,1)} %get-tuple-element.9, bf16[40,1,1024]{2,1,0:T(2,128)(2,1)S(1)} %get-tuple-element.8, bf16[40,64,1024]{2,1,0:T(8,128)(2,1)} %get-tuple-element.10), kind=kLoop, calls=%fused_computation.4 | loop fusion | flops 21299200 | bytes 21299200 | tf_op jit(solution)/shard_map/concatenate | solution.py:57
  90.4 9.1 %reshape.86 = bf16[40,65,8,128]{3,2,1,0:T(8,128)(2,1)} reshape(bf16[40,65,1024]{2,1,0:T(8,128)(2,1)} %get-tuple-element.11) | data formatting | bytes 10649600 | tf_op jit(solution)/shard_map/reshape | solution.py:63
  99.5 9.3 %reshape.87 = bf16[40,65,8,128]{3,2,1,0:T(8,128)(2,1)} reshape(bf16[40,65,1024]{2,1,0:T(8,128)(2,1)} %get-tuple-element.12) | data formatting | bytes 10649600 | tf_op jit(solution)/shard_map/reshape | solution.py:64
  108.8 5.9 %fusion.4 = f32[40,8,1,65]{3,2,1,0:T(1,128)S(1)} fusion(bf16[40,65,8,128]{3,2,1,0:T(8,128)(2,1)} %reshape.86, bf16[40,3,1024]{2,1,0:T(4,128)(2,1)S(1)} %reshape.54), kind=kOutput, calls=%fused_computation.8 | convolution fusion | flops 5324800 | bytes 5571840 | tf_op jit(solution)/shard_map/thd,tjhd->thj/dot_general | solution.py:66
  114.6 0.2 fusion.10
  114.9 4.2 %fusion.2 = f32[40,8,1,128]{3,2,1,0:T(1,128)S(1)} fusion(bf16[40,65,8,128]{3,2,1,0:T(8,128)(2,1)} %reshape.87, bf16[40,8,65,1]{2,1,0,3:T(8,128)(2,1)S(1)} %fusion.10), kind=kOutput, calls=%fused_computation.6 | convolution fusion | flops 5324800 | bytes 5530240 | tf_op jit(solution)/shard_map/thj,tjhd->thd/dot_general | solution.py:70
  119.1 16.2 %all-gather.2.cloned.1.call-done = bf16[1024,4096]{1,0:T(8,128)(2,1)} async-done(((bf16[1024,512]{1,0:T(8,128)(2,1)}), bf16[1024,4096]{1,0:T(8,128)(2,1)}) %all-gather.2.cloned.1.call-update) | async-done | bytes 8388624 | tf_op jit(solution)/shard_map/all_gather | solution.py:76
  135.3 0.0 copy-start.2
  135.3 5.9 %fusion.19 = f32[40,4096]{1,0:T(8,128)} fusion(bf16[1024,4096]{1,0:T(8,128)(2,1)} %all-gather.2.cloned.1.call-done, bf16[5,8,8,128]{3,2,1,0:T(8,128)(2,1)S(1)} %bitcast.36), kind=kOutput, calls=%fused_computation.34 | convolution fusion | flops 335544320 | bytes 9125888 | tf_op jit(solution)/shard_map/dot_general | solution.py:74
  141.2 0.0 all-reduce.2.cloned.1.call-update
  141.2 0.0 reduce-scatter.7.cloned.1.call-start
  141.3 0.0 copy-done.2
  141.3 0.1 copy.27
  141.4 0.7 dynamic-slice
  142.1 39.9 %all-reduce.2.cloned.1.call-done = f32[40,4096]{1,0:T(8,128)} async-done(((f32[40,4096]{1,0:T(8,128)}), f32[40,4096]{1,0:T(8,128)}) %all-reduce.2.cloned.1.call-update) | async-done | bytes 655376 | tf_op jit(solution)/shard_map/psum | solution.py:79
  181.9 0.0 copy-done.1
  181.9 1.3 multiply_reduce_fusion
  183.2 0.0 copy-done
  183.2 0.5 convolution_bitcast_fusion
  183.8 0.3 convolution_convert_fusion
  184.1 0.7 copy.40
  184.9 0.0 reduce-scatter.7.cloned.1.call-update
  184.9 0.8 convert_element_type.37
  185.7 18.2 %reduce-scatter.7.cloned.1.call-done = bf16[64,40]{1,0:T(8,128)(2,1)} async-done(((bf16[256,40]{1,0:T(8,128)(2,1)}), bf16[64,40]{1,0:T(8,128)(2,1)}) %reduce-scatter.7.cloned.1.call-update) | async-done | bytes 5136
  203.9 0.8 copy.39
  204.7 0.6 convert_element_type.41
  (7 shorter events, 0.1 us)
Async XLA Ops:
  7.2 176.1 %copy-start = (bf16[1024,1024]{1,0:T(8,128)(2,1)S(1)}, bf16[1024,1024]{1,0:T(8,128)(2,1)}, u32[]{:S(2)}) copy-start(bf16[1024,1024]{1,0:T(8,128)(2,1)} %param.17) | copy-start | bytes 6291460
  10.4 12.8 %all-to-all-start = ((bf16[40,8,512]{2,0,1:T(8,128)(2,1)}), bf16[40,8,512]{2,0,1:T(8,128)(2,1)S(1)}, u32[]{:S(2)}, u32[]{:S(2)}) async-start(bf16[40,8,512]{2,0,1:T(8,128)(2,1)} %bitcast.32), calls=%async_computation | async-start | bytes 655360 | tf_op jit(solution)/shard_map/all_to_all | solution.py:43
  15.6 62.0 %reduce-scatter.5.cloned.1.call-start = ((), (), s32[]{:S(2)}) async-start(), calls=%async_computation.3 | async-start | bytes 4423680 | tf_op jit(solution)/shard_map/reduce_scatter | solution.py:47
  23.2 5.8 %copy-start.3 = (s32[40]{0:T(128)S(1)}, s32[40]{0:T(128)}, u32[]{:S(2)}) copy-start(s32[40]{0:T(128)} %param.20) | copy-start | bytes 484
  28.2 107.1 %all-gather.2.cloned.1.call-start = ((), (), s32[]{:S(2)}) async-start(), calls=%async_computation.4 | async-start | bytes 9437184 | tf_op jit(solution)/shard_map/all_gather | solution.py:76
  29.0 153.0 %all-reduce.2.cloned.1.call-start = ((), (), s32[]{:S(2)}) async-start(), calls=%async_computation.5 | async-start | bytes 1310720 | tf_op jit(solution)/shard_map/psum | solution.py:79
  135.3 6.0 %copy-start.2 = (s32[40,2]{0,1:T(2,128)S(1)}, s32[40,2]{0,1:T(2,128)}, u32[]{:S(2)}) copy-start(s32[40,2]{0,1:T(2,128)} %param.21) | copy-start | bytes 964
  135.3 46.6 %copy-start.1 = (bf16[40,4096]{1,0:T(8,128)(2,1)S(1)}, bf16[40,4096]{1,0:T(8,128)(2,1)}, u32[]{:S(2)}) copy-start(bf16[40,4096]{1,0:T(8,128)(2,1)} %param.12) | copy-start | bytes 983044
  141.2 62.7 %reduce-scatter.7.cloned.1.call-start = ((), (), s32[]{:S(2)}) async-start(), calls=%async_computation.6 | async-start | bytes 81920
Sparse Core Ops, SparseCore 0:
  28.3 49.1 reduce-scatter.4
  79.4 55.8 all-gather.1
  141.4 40.5 all-reduce.1
  185.0 18.8 reduce-scatter.6
where the time goes:
time: 213 us; the launch traced here: 212 us
  waiting for transfers between devices  103 us (48%)
  local copies, waits for them, and re-layouts  41.6 us (20%)
  other arithmetic  26.6 us (12%)
  matrix products  21.8 us (10%)
  between operations  13.9 us (7%)
  starting transfers between devices  5.36 us (3%)
    psum x1, waiting for transfers between devices, on_device(): attn_out = lax.psum(partial_value, 'mp')  39.9 us
    reduce_scatter x1, waiting for transfers between devices, on_device(): lax.psum_scatter(jnp.dot(spread, flat_qkv, preferred_element_type=jnp.flo...  24.6 us
    unnamed x5, waiting for transfers between devices  19 us
    all_gather x1, waiting for transfers between devices, on_device(): lax.all_gather(out_weight, 'dp', axis=1, tiled=True)  16.2 us
    concatenate x1, other arithmetic, on_device(): jnp.concatenate([jnp.take(key_cache, source, axis=0), projected[:, 1][:,...  11.1 us
    reshape x1, local copies, waits for them, and re-layouts, on_device(): value_rows = value_rows.reshape(row_count, length, local_heads, HEAD)  9.25 us
    reshape x1, local copies, waits for them, and re-layouts, on_device(): key_rows = key_rows.reshape(row_count, length, local_heads, HEAD)  9.11 us
    select_n x1, other arithmetic, on_device(): jnp.take(key_cache, source, axis=0)  9.08 us
  transfers between devices with their start and end apart: 5, of which 5 were waited for; matrix products, arithmetic and copies ran while one was open for 34% of the time, Pallas kernels for 0%

commit v1 on v0

--- a/solution.py
+++ b/solution.py
@@ -73,7 +73,9 @@
     attention_result = attention_result.astype(jnp.bfloat16).reshape(row_count, head_width)
     partial_value = jnp.dot(
         attention_result,
-        lax.all_gather(out_weight, "dp", axis=1, tiled=True),
+        jnp.concatenate(
+            lax.all_to_all(jnp.stack([out_weight] * lax.axis_size("dp")), "dp", 0, 0), axis=1
+        ),
         preferred_element_type=jnp.float32,
     )
     attn_out = lax.psum(partial_value, "mp")

time: 213 us -> 249 us (1.17)
  waiting for transfers between devices: 103 us -> 127 us
  starting transfers between devices: 5.36 us -> 10.7 us
  local copies, waits for them, and re-layouts: 41.6 us -> 46.9 us
    reduce_scatter x1, waiting for transfers between devices: 24.6 us -> 47.6 us  [on_device(): lax.psum_scatter(jnp.dot(spread, flat_qkv, preferred_element_type=jnp.flo...]
    psum x1, waiting for transfers between devices: 39.9 us -> 58.4 us  [on_device(): attn_out = lax.psum(partial_value, 'mp')]
    all_gather x1 -> x0, waiting for transfers between devices: 16.2 us -> none  [on_device(): lax.all_gather(out_weight, 'dp', axis=1, tiled=True)]
    all_to_all x0 -> x1, starting transfers between devices: none -> 5.18 us  [on_device(): lax.all_to_all(jnp.stack([out_weight] * lax.axis_size('dp')), 'dp', 0, 0)]
    another operation x0 -> x1, local copies, waits for them, and re-layouts: none -> 4.3 us  [on_device(): jnp.stack([out_weight] * lax.axis_size('dp'))]
    unnamed x13 -> x14, local copies, waits for them, and re-layouts: 6.34 us -> 7.84 us
    unnamed x5 -> x4, waiting for transfers between devices: 19 us -> 18.3 us
  transfers between devices with their start and end apart: 5 -> 5, of which waited for: 5 -> 4; matrix products, arithmetic and copies ran while one was open for 34% -> 31% of each run, Pallas kernels for 0% -> 0%
where the time goes in v1:
time: 249 us; the launch traced here: 248 us
  waiting for transfers between devices  127 us (51%)
  local copies, waits for them, and re-layouts  46.9 us (19%)
  other arithmetic  26.3 us (11%)
  matrix products  22.6 us (9%)
  between operations  13.9 us (6%)
  starting transfers between devices  10.7 us (4%)
    psum x1, waiting for transfers between devices, on_device(): attn_out = lax.psum(partial_value, 'mp')  58.4 us
    reduce_scatter x1, waiting for transfers between devices, on_device(): lax.psum_scatter(jnp.dot(spread, flat_qkv, preferred_element_type=jnp.flo...  47.6 us
    unnamed x4, waiting for transfers between devices  18.3 us
    concatenate x1, other arithmetic, on_device(): jnp.concatenate([jnp.take(key_cache, source, axis=0), projected[:, 1][:,...  11 us
    reshape x1, local copies, waits for them, and re-layouts, on_device(): key_rows = key_rows.reshape(row_count, length, local_heads, HEAD)  9.11 us
    reshape x1, local copies, waits for them, and re-layouts, on_device(): value_rows = value_rows.reshape(row_count, length, local_heads, HEAD)  9.09 us
    select_n x1, other arithmetic, on_device(): jnp.take(key_cache, source, axis=0)  8.92 us
    unnamed x14, local copies, waits for them, and re-layouts  7.84 us
  transfers between devices with their start and end apart: 5, of which 4 were waited for; matrix products, arithmetic and copies ran while one was open for 31% of the time, Pallas kernels for 0%

profile of v1, /device:TPU:0, one launch (start us, length us, event | category | flops | bytes accessed | tf_op | source)
XLA Modules:
  0.0 247.7 jit_solution(12631220784893852910)
XLA Ops:
  7.2 0.0 copy-start
  7.2 1.3 fusion.11
  8.5 1.1 fusion.13
  9.6 0.7 copy.58
  10.4 5.2 %all-to-all-start = ((bf16[40,8,512]{2,0,1:T(8,128)(2,1)}), bf16[40,8,512]{2,0,1:T(8,128)(2,1)S(1)}, u32[]{:S(2)}, u32[]{:S(2)}) async-start(bf16[40,8,512]{2,0,1:T(8,128)(2,1)} %bitcast.35), calls=%async_computation | async-start | bytes 655360 | tf_op jit(solution)/shard_map/all_to_all | solution.py:43
  15.6 0.0 reduce-scatter.5.cloned.1.call-start
  15.6 4.7 %copy.26 = bf16[512,3,1024]{0,2,1:T(8,128)(2,1)} copy(bf16[512,3,1024]{2,0,1:T(8,128)(2,1)} %param.15) | data formatting | bytes 6291456 | tf_op args[3]
  20.3 2.9 %all-to-all-done = bf16[40,8,512]{2,0,1:T(8,128)(2,1)S(1)} async-done(((bf16[40,8,512]{2,0,1:T(8,128)(2,1)}), bf16[40,8,512]{2,0,1:T(8,128)(2,1)S(1)}, u32[]{:S(2)}, u32[]{:S(2)}) %all-to-all-start) | async-done | bytes 327712 | tf_op jit(solution)/shard_map/all_to_all | solution.py:43
  23.2 5.0 %fusion.35 = f32[320,3072]{1,0:T(8,128)} fusion(bf16[320,512]{1,0:T(8,128)(2,1)S(1)} %bitcast.37, bf16[512,3072]{0,1:T(8,128)(2,1)} %bitcast.36), kind=kOutput, calls=%fused_computation.57 | convolution fusion | flops 1006632960 | bytes 7405568 | tf_op jit(solution)/shard_map/dot_general | solution.py:48
  28.1 0.0 reduce-scatter.5.cloned.1.call-update
  28.2 1.5 copy.29
  29.7 4.3 %stack.2 = bf16[8,1024,512]{1,2,0:T(8,128)(2,1)} broadcast(bf16[1024,512]{0,1:T(8,128)(2,1)S(1)} %copy.29), dimensions={1,2} | broadcast | bytes 9437184 | tf_op jit(solution)/shard_map/stack | solution.py:77
  34.0 5.2 %all-to-all-start.1 = ((bf16[8,1024,512]{1,2,0:T(8,128)(2,1)}), bf16[8,1024,512]{1,2,0:T(8,128)(2,1)}, u32[]{:S(2)}, u32[]{:S(2)}) async-start(bf16[8,1024,512]{1,2,0:T(8,128)(2,1)} %stack.2), calls=%async_computation.2 | async-start | bytes 16777216 | tf_op jit(solution)/shard_map/all_to_all | solution.py:77
  39.2 0.2 all-reduce.2.cloned.1.call-start
  39.4 0.0 copy-done.3
  39.4 7.4 %gather_fusion = bf16[40,64,1024]{2,1,0:T(8,128)(2,1)} fusion(bf16[40,64,1024]{2,1,0:T(8,128)(2,1)} %param.18, s32[1024]{0:T(1024)S(1)} %pad_clamp_fusion), kind=kCustom, calls=%fused_computation.clone | custom fusion | bytes 10485920 | tf_op jit(solution)/shard_map/jit(_take)/gather | solution.py:58
  46.9 7.1 %gather_fusion.1 = bf16[40,64,1024]{2,1,0:T(8,128)(2,1)} fusion(bf16[40,64,1024]{2,1,0:T(8,128)(2,1)} %param.19, s32[1024]{0:T(1024)S(1)} %pad_clamp_fusion), kind=kCustom, calls=%fused_computation.1.clone | custom fusion | bytes 10485920 | tf_op jit(solution)/shard_map/jit(_take)/gather | solution.py:61
  54.0 8.9 %broadcast_select_fusion.1 = (bf16[40,64,1024]{2,1,0:T(8,128)(2,1)}, bf16[40,64,1024]{2,1,0:T(8,128)(2,1)}) fusion(bf16[40,64,1024]{2,1,0:T(8,128)(2,1)} %gather_fusion, pred[40]{0:T(512)(128)(4,1)S(1)} %get-tuple-element.5, bf16[40,64,1024]{2,1,0:T(8,128)(2,1)} %gather_fusion.1), kind=kLoop, calls=%fused_computation.11 | loop fusion | flops 5242880 | bytes 20971560 | tf_op jit(solution)/shard_map/jit(_take)/select_n | solution.py:58
  62.9 47.6 %reduce-scatter.5.cloned.1.call-done = f32[40,3072]{1,0:T(8,128)} async-done(((f32[320,3072]{1,0:T(8,128)}), f32[40,3072]{1,0:T(8,128)}) %reduce-scatter.5.cloned.1.call-update) | async-done | bytes 491536 | tf_op jit(solution)/shard_map/reduce_scatter | solution.py:47
  110.5 1.1 convert_element_type.34
  111.5 0.4 reshape.62
  111.9 0.3 fusion.32
  112.2 11.0 %pad_maximum_fusion = (bf16[40,65,1024]{2,1,0:T(8,128)(2,1)}, bf16[40,65,1024]{2,1,0:T(8,128)(2,1)}) fusion(bf16[40,1,1024]{2,1,0:T(2,128)(2,1)S(1)} %get-tuple-element.7, bf16[40,64,1024]{2,1,0:T(8,128)(2,1)} %get-tuple-element.9, bf16[40,1,1024]{2,1,0:T(2,128)(2,1)S(1)} %get-tuple-element.8, bf16[40,64,1024]{2,1,0:T(8,128)(2,1)} %get-tuple-element.10), kind=kLoop, calls=%fused_computation.4 | loop fusion | flops 21299200 | bytes 21299200 | tf_op jit(solution)/shard_map/concatenate | solution.py:57
  123.2 9.1 %reshape.96 = bf16[40,65,8,128]{3,2,1,0:T(8,128)(2,1)} reshape(bf16[40,65,1024]{2,1,0:T(8,128)(2,1)} %get-tuple-element.11) | data formatting | bytes 10649600 | tf_op jit(solution)/shard_map/reshape | solution.py:63
  132.3 9.1 %reshape.97 = bf16[40,65,8,128]{3,2,1,0:T(8,128)(2,1)} reshape(bf16[40,65,1024]{2,1,0:T(8,128)(2,1)} %get-tuple-element.12) | data formatting | bytes 10649600 | tf_op jit(solution)/shard_map/reshape | solution.py:64
  141.4 5.6 %fusion.4 = f32[40,8,1,65]{3,2,1,0:T(1,128)S(1)} fusion(bf16[40,65,8,128]{3,2,1,0:T(8,128)(2,1)} %reshape.96, bf16[40,3,1024]{2,1,0:T(4,128)(2,1)S(1)} %reshape.62), kind=kOutput, calls=%fused_computation.8 | convolution fusion | flops 5324800 | bytes 5571840 | tf_op jit(solution)/shard_map/thd,tjhd->thj/dot_general | solution.py:66
  147.1 0.2 fusion.10
  147.3 4.2 %fusion.2 = f32[40,8,1,128]{3,2,1,0:T(1,128)S(1)} fusion(bf16[40,65,8,128]{3,2,1,0:T(8,128)(2,1)} %reshape.97, bf16[40,8,65,1]{2,1,0,3:T(8,128)(2,1)S(1)} %fusion.10), kind=kOutput, calls=%fused_computation.6 | convolution fusion | flops 5324800 | bytes 5530240 | tf_op jit(solution)/shard_map/thj,tjhd->thd/dot_general | solution.py:70
  151.5 0.0 copy-start.2
  151.6 0.0 all-to-all-done.1
  151.6 6.9 %fusion.19 = f32[40,4096]{1,0:T(8,128)} fusion(bf16[1024,4096]{0,1:T(8,128)(2,1)} %bitcast.10, bf16[5,8,8,128]{3,2,1,0:T(8,128)(2,1)S(1)} %bitcast.39), kind=kOutput, calls=%fused_computation.34 | convolution fusion | flops 335544320 | bytes 9125888 | tf_op jit(solution)/shard_map/dot_general | solution.py:74
  158.5 0.0 all-reduce.2.cloned.1.call-update
  158.5 0.0 reduce-scatter.7.cloned.1.call-start
  158.6 0.0 copy-done.2
  158.6 0.1 copy.30
  158.7 0.7 dynamic-slice
  159.4 58.4 %all-reduce.2.cloned.1.call-done = f32[40,4096]{1,0:T(8,128)} async-done(((f32[40,4096]{1,0:T(8,128)}), f32[40,4096]{1,0:T(8,128)}) %all-reduce.2.cloned.1.call-update) | async-done | bytes 655376 | tf_op jit(solution)/shard_map/psum | solution.py:81
  217.8 0.0 copy-done.1
  217.8 1.3 multiply_reduce_fusion
  219.1 0.0 copy-done
  219.1 0.5 convolution_bitcast_fusion
  219.7 0.3 convolution_convert_fusion
  220.0 0.7 copy.43
  220.8 0.0 reduce-scatter.7.cloned.1.call-update
  220.8 0.8 convert_element_type.37
  221.5 18.2 %reduce-scatter.7.cloned.1.call-done = bf16[64,40]{1,0:T(8,128)(2,1)} async-done(((bf16[256,40]{1,0:T(8,128)(2,1)}), bf16[64,40]{1,0:T(8,128)(2,1)}) %reduce-scatter.7.cloned.1.call-update) | async-done | bytes 5136
  239.8 0.8 copy.42
  240.6 0.6 convert_element_type.41
  (8 shorter events, 0.1 us)
Async XLA Ops:
  7.2 212.0 %copy-start = (bf16[1024,1024]{1,0:T(8,128)(2,1)S(1)}, bf16[1024,1024]{1,0:T(8,128)(2,1)}, u32[]{:S(2)}) copy-start(bf16[1024,1024]{1,0:T(8,128)(2,1)} %param.17) | copy-start | bytes 6291460
  10.4 12.8 %all-to-all-start = ((bf16[40,8,512]{2,0,1:T(8,128)(2,1)}), bf16[40,8,512]{2,0,1:T(8,128)(2,1)S(1)}, u32[]{:S(2)}, u32[]{:S(2)}) async-start(bf16[40,8,512]{2,0,1:T(8,128)(2,1)} %bitcast.35), calls=%async_computation | async-start | bytes 655360 | tf_op jit(solution)/shard_map/all_to_all | solution.py:43
  15.6 94.9 %reduce-scatter.5.cloned.1.call-start = ((), (), s32[]{:S(2)}) async-start(), calls=%async_computation.4 | async-start | bytes 4423680 | tf_op jit(solution)/shard_map/reduce_scatter | solution.py:47
  34.0 5.4 %copy-start.3 = (s32[40]{0:T(128)S(1)}, s32[40]{0:T(128)}, u32[]{:S(2)}) copy-start(s32[40]{0:T(128)} %param.20) | copy-start | bytes 484
  34.0 117.6 %all-to-all-start.1 = ((bf16[8,1024,512]{1,2,0:T(8,128)(2,1)}), bf16[8,1024,512]{1,2,0:T(8,128)(2,1)}, u32[]{:S(2)}, u32[]{:S(2)}) async-start(bf16[8,1024,512]{1,2,0:T(8,128)(2,1)} %stack.2), calls=%async_computation.2 | async-start | bytes 16777216 | tf_op jit(solution)/shard_map/all_to_all | solution.py:77
  39.2 178.7 %all-reduce.2.cloned.1.call-start = ((), (), s32[]{:S(2)}) async-start(), calls=%async_computation.5 | async-start | bytes 1310720 | tf_op jit(solution)/shard_map/psum | solution.py:81
  151.5 7.1 %copy-start.2 = (s32[40,2]{0,1:T(2,128)S(1)}, s32[40,2]{0,1:T(2,128)}, u32[]{:S(2)}) copy-start(s32[40,2]{0,1:T(2,128)} %param.21) | copy-start | bytes 964
  151.5 66.3 %copy-start.1 = (bf16[40,4096]{1,0:T(8,128)(2,1)S(1)}, bf16[40,4096]{1,0:T(8,128)(2,1)}, u32[]{:S(2)}) copy-start(bf16[40,4096]{1,0:T(8,128)(2,1)} %param.12) | copy-start | bytes 983044
  158.5 81.2 %reduce-scatter.7.cloned.1.call-start = ((), (), s32[]{:S(2)}) async-start(), calls=%async_computation.6 | async-start | bytes 81920
Sparse Core Ops, SparseCore 0:
  28.3 82.1 reduce-scatter.4
  158.7 59.1 all-reduce.1
  220.9 18.8 reduce-scatter.6
